TPU v7x, 128 devices: a whole 4x4x4 slice. The times are simulated.
128 devices in a mesh: heads: 8 (over z, core), width: 4 (over y), sae: 4 (over x).
Axes of the slice: x: 4, y: 4, z: 4, core: 2. Of those that a mesh axis runs over, the one named last changes fastest.
Arguments:
- x_in: bfloat16 [512, 4608], P(None, 'width'), may hold values from -64 to 64
- doc_lengths: int32 [4], replicated, may hold values from 1 to 256, 512 in all
- attn_gain: float32 [4608], P('width'), may hold values from 0.25 to 1.75
- w_query: bfloat16 [4608, 4096], P('width', 'heads'), may hold values from -0.09375 to 0.09375
- w_key: bfloat16 [4608, 2048], P('width', 'heads'), may hold values from -0.09375 to 0.09375
- w_value: bfloat16 [4608, 2048], P('width', 'heads'), may hold values from -0.09375 to 0.09375
- w_out: bfloat16 [4096, 4608], P('heads', 'width'), may hold values from -0.09375 to 0.09375
- post_gain: float32 [4608], replicated, may hold values from 0.25 to 1.75
- enc_weight: bfloat16 [4608, 65536], P(None, ('heads', 'width', 'sae')), may hold values from -0.09375 to 0.09375
- enc_bias: float32 [65536], P(('heads', 'width', 'sae')), may hold values from -1.5 to 0.5
- dec_weight: bfloat16 [65536, 4608], P(('heads', 'width', 'sae')), may hold values from -1 to 1
- dec_bias: float32 [4608], replicated, may hold values from -5 to 5
Outputs:
- grad_enc: bfloat16 [4608, 65536], P(None, ('heads', 'width', 'sae'))
- grad_dec: bfloat16 [65536, 4608], P(('heads', 'width', 'sae'))
- total_loss: float32 [], replicated
Inputs may be any that keep to these rules, and one draw needn't show every extreme that they name: `doc_lengths`: lengths of the 4 documents packed in order; they sum to 512.
All inputs are finite; a program needn't handle non-finite values.
Results may differ from a plain program's by a relative error of at most 0.02.
Values may be sent and summed in bfloat16 or wider, within the bound.
A program may use at most 128 MiB of HBM per device.

v0:
```python
import jax
import jax.numpy as jnp
from jax import lax
from jax.sharding import PartitionSpec as P

D = 4608
HEADS = 32
HEAD_DIM = 128
norm_eps = 1e-06
soft_cap = 50.0
rope_base = 10000.0
l1_weight = 3.0


def rotary(values, position):
    half_dim = values.shape[-1] // 2
    frequency = rope_base ** (-2.0 * jnp.arange(half_dim, dtype=jnp.float32) / values.shape[-1])
    angles = position.astype(jnp.float32)[:, None] * frequency[None, :]
    cosine_table = jnp.cos(angles)[:, None, :]
    sine_table = jnp.sin(angles)[:, None, :]
    first_half = values[..., :half_dim]
    second_half = values[..., half_dim:]
    return jnp.concatenate(
        [
            first_half * cosine_table - second_half * sine_table,
            second_half * cosine_table + first_half * sine_table,
        ],
        axis=-1,
    )


def attend_rows(query_rows, key_rows, value_rows, allowed_rows, scale):
    scores = (
        jnp.einsum("tkgd,skd->kgts", query_rows, key_rows, preferred_element_type=jnp.float32)
        * scale
    )
    capped = soft_cap * jnp.tanh(scores / soft_cap)
    weights = jnp.where(allowed_rows[None, None], jnp.exp(capped), 0.0)
    totals = jnp.sum(weights, axis=-1, keepdims=True)
    probs_bf = (weights / totals).astype(jnp.bfloat16)
    return jnp.einsum(
        "kgts,skd->tkgd", probs_bf, value_rows, preferred_element_type=jnp.float32
    ).astype(jnp.bfloat16)


def per_device(
    x_in,
    doc_lengths,
    attn_gain,
    w_query,
    w_key,
    w_value,
    w_out,
    post_gain,
    enc_weight,
    enc_bias,
    dec_weight,
    dec_bias,
):
    tokens = x_in.shape[0]
    query_heads = w_query.shape[1] // HEAD_DIM
    value_heads = w_key.shape[1] // HEAD_DIM
    boundary = jnp.cumsum(doc_lengths)
    position = jnp.arange(tokens, dtype=jnp.int32)
    segment = jnp.sum((boundary[None, :] <= position[:, None]).astype(jnp.int32), axis=1)
    allowed = (segment[:, None] == segment[None, :]) & (position[None, :] <= position[:, None])
    x_float = x_in.astype(jnp.float32)
    scaled = (x_float * attn_gain).astype(jnp.bfloat16)
    query_part = jnp.dot(scaled, w_query, preferred_element_type=jnp.float32)
    key_part = jnp.dot(scaled, w_key, preferred_element_type=jnp.float32)
    value_part = jnp.dot(scaled, w_value, preferred_element_type=jnp.float32)
    square_part = jnp.sum(x_float * x_float, axis=1)
    query_raw, key_raw, value_raw, square_sums = lax.psum(
        (query_part, key_part, value_part, square_part), "width"
    )
    inverse_rms = lax.rsqrt(square_sums / D + norm_eps)
    query = rotary(
        (query_raw * inverse_rms[:, None]).reshape(tokens, query_heads, HEAD_DIM), position
    ).astype(jnp.bfloat16)
    key_rows = rotary(
        (key_raw * inverse_rms[:, None]).reshape(tokens, value_heads, HEAD_DIM), position
    ).astype(jnp.bfloat16)
    value_rows = (
        (value_raw * inverse_rms[:, None])
        .reshape(tokens, value_heads, HEAD_DIM)
        .astype(jnp.bfloat16)
    )
    query4 = query.reshape(tokens, value_heads, query_heads // value_heads, HEAD_DIM)
    pieces_out = attend_rows(query4, key_rows, value_rows, allowed, (D // HEADS) ** (-0.5))
    mixed = pieces_out.reshape(tokens, query_heads * HEAD_DIM)
    proj_part = jnp.dot(mixed, w_out, preferred_element_type=jnp.float32)
    attn_sum = lax.psum(proj_part, "heads")
    attn_local = attn_sum.astype(jnp.bfloat16)
    attn_proj, x_full = (
        lax.all_gather(attn_local, "width", axis=1, tiled=True),
        lax.all_gather(x_in, "width", axis=1, tiled=True),
    )
    proj_float = attn_proj.astype(jnp.float32)
    inverse_post = lax.rsqrt(jnp.sum(proj_float * proj_float, axis=1) / D + norm_eps)
    resid = (x_full.astype(jnp.float32) + proj_float * inverse_post[:, None] * post_gain).astype(
        jnp.bfloat16
    )
    centered = (resid.astype(jnp.float32) - dec_bias).astype(jnp.bfloat16)
    pre_acts = jnp.dot(centered, enc_weight, preferred_element_type=jnp.float32) + enc_bias
    latent_acts = jnp.maximum(pre_acts, 0.0).astype(jnp.bfloat16)
    row_norms = jnp.sqrt(jnp.sum(jnp.square(dec_weight.astype(jnp.float32)), axis=1) + norm_eps)
    act_sums = jnp.sum(latent_acts.astype(jnp.float32), axis=0)
    penalty_part = jnp.sum(act_sums * row_norms)
    recon_part = jnp.dot(latent_acts, dec_weight, preferred_element_type=jnp.float32)
    recon = lax.psum(recon_part, ("heads", "width", "sae")) + dec_bias
    error = recon - resid.astype(jnp.float32)
    squares_total = jnp.sum(error * error)
    penalty_total = lax.psum(penalty_part, ("heads", "width", "sae"))
    grad_recon = (2.0 / tokens * error).astype(jnp.bfloat16)
    total_loss = (squares_total + l1_weight * penalty_total) / (tokens * D)
    upstream = lax.dot_general(
        grad_recon, dec_weight, (((1,), (1,)), ((), ())), preferred_element_type=jnp.float32
    )
    grad_pre = jnp.where(pre_acts > 0, upstream + l1_weight * row_norms / tokens, 0.0).astype(
        jnp.bfloat16
    )
    grad_enc = lax.dot_general(
        centered, grad_pre, (((0,), (0,)), ((), ())), preferred_element_type=jnp.float32
    ).astype(jnp.bfloat16)
    decoder_term = lax.dot_general(
        latent_acts, grad_recon, (((0,), (0,)), ((), ())), preferred_element_type=jnp.float32
    )
    grad_dec = (
        decoder_term
        + l1_weight
        / tokens
        * act_sums[:, None]
        * dec_weight.astype(jnp.float32)
        / row_norms[:, None]
    ).astype(jnp.bfloat16)
    return (grad_enc, grad_dec, total_loss)


def solution(mesh):
    placed = (
        P(None, "width"),
        P(),
        P("width"),
        P("width", "heads"),
        P("width", "heads"),
        P("width", "heads"),
        P("heads", "width"),
        P(),
        P(None, ("heads", "width", "sae")),
        P(("heads", "width", "sae")),
        P(("heads", "width", "sae"), None),
        P(),
    )
    return jax.shard_map(
        per_device,
        mesh=mesh,
        in_specs=placed,
        out_specs=(P(None, ("heads", "width", "sae")), P(("heads", "width", "sae"), None), P()),
        check_vma=False,
    )
```

profile of v0, /device:TPU:1, one launch (start us, length us, event | category | flops | bytes accessed | tf_op | source)
XLA Modules:
  0.0 471.6 jit_solution(9375944868353371698)
XLA Ops:
  7.2 0.0 copy-start
  7.2 0.0 all-reduce.7.cloned.1.call-start
  7.3 3.6 fusion.23
  10.9 2.7 fusion.25
  13.6 1.3 fusion.27
  14.9 0.0 all-reduce.7.cloned.1.call-update
  15.0 0.0 all-gather.5.cloned.1.call-start
  15.0 0.2 reduce-window.8
  15.2 0.3 fusion.14
  15.5 9.5 %psum.50 = f32[512]{0:T(512)S(1)} all-reduce(f32[512]{0:T(512)S(1)} %fusion.14), channel_id=1, replica_groups=mesh['heads'=8,'width'=4,'sae'=4] {'width'}, use_global_device_ids=true, to_apply=%region_2.3 | all-reduce | flops 512 | bytes 4096 | tf_op jit(solution)/shard_map/psum | solution.py:73
  25.1 0.1 convert_reduce_fusion.1
  25.2 0.9 fusion.22
  26.1 1.7 multiply_cosine_fusion
  27.8 49.0 %all-reduce.7.cloned.1.call-done = (f32[512,256]{1,0:T(8,128)}, f32[512,512]{1,0:T(8,128)}, f32[512,256]{1,0:T(8,128)}) async-done(((f32[512,256]{1,0:T(8,128)}, f32[512,512]{1,0:T(8,128)}, f32[512,256]{1,0:T(8,128)}), (f32[512,256]{1,0:T(8,128)}, f32[512,512]{1,0:T(8,128)}, f32[512,256]{1,0:T(8,128)})) %all-reduce.7.cloned.1.call-update) | async-done | bytes 2097168 | tf_op jit(solution)/shard_map/psum | solution.py:73
  76.9 2.1 broadcast_multiply_fusion.1
  78.9 0.3 reshape.168
  79.2 1.5 fusion.40
  80.7 1.4 broadcast_multiply_fusion
  82.1 0.4 reshape.169
  82.5 1.8 subtract_convert_fusion
  84.3 0.1 copy.23
  84.3 0.1 copy.24
  84.4 0.1 copy.30
  84.6 1.3 subtract_convert_fusion.1
  85.9 2.9 fusion.12
  88.8 1.6 fusion.21
  90.4 0.9 fusion.41
  91.3 52.5 %all-reduce.8 = bf16[512,1152]{1,0:T(8,128)(2,1)} all-reduce(f32[512,1152]{1,0:T(8,128)S(1)} %fusion.41), channel_id=1, replica_groups=mesh['heads'=8,'width'=4,'sae'=4] {'heads'}, use_global_device_ids=true, to_apply=%region_8.9 | all-reduce | flops 589824 | bytes 3538944 | tf_op jit(solution)/shard_map/psum | solution.py:92
  143.8 0.0 all-gather.5.cloned.1.call-update
  143.8 0.0 all-gather.3.cloned.1.call-start
  143.8 0.7 all-gather.3.cloned.1.call-update
  144.5 0.2 all-reduce.5.cloned.1.call-start
  144.8 51.8 %all-gather.5.cloned.1.call-done = bf16[512,4608]{1,0:T(8,128)(2,1)} async-done(((bf16[512,1152]{1,0:T(8,128)(2,1)}), bf16[512,4608]{1,0:T(8,128)(2,1)}) %all-gather.5.cloned.1.call-update) | async-done | bytes 4718608 | tf_op jit(solution)/shard_map/all_gather | solution.py:95
  196.6 3.3 fusion
  200.0 51.3 %all-gather.3.cloned.1.call-done = bf16[512,4608]{1,0:T(8,128)(2,1)} async-done(((bf16[512,1152]{1,0:T(8,128)(2,1)}), bf16[512,4608]{1,0:T(8,128)(2,1)}) %all-gather.3.cloned.1.call-update) | async-done | bytes 4718608 | tf_op jit(solution)/shard_map/all_gather | solution.py:96
  251.3 5.9 %fusion.3 = bf16[512,4608]{1,0:T(8,128)(2,1)S(1)} fusion(bf16[512,4608]{1,0:T(8,128)(2,1)} %all-gather.5.cloned.1.call-done, bf16[512,4608]{1,0:T(8,128)(2,1)} %all-gather.3.cloned.1.call-done, f32[4608]{0:T(1024)S(1)} %copy-done.8, f32[512]{0:T(512)S(1)} %add_rsqrt_fusion), kind=kLoop, calls=%fused_computation.9 | loop fusion | flops 14155776 | bytes 14176256 | tf_op jit(solution)/shard_map/convert_element_type | solution.py:100
  257.2 0.0 slice-start.1
  257.3 6.4 %convert_reduce_fusion = (f32[512]{0:T(512)S(1)}, f32[512,512]{1,0:T(8,128)S(1)}) fusion(f32[512]{0:T(512)S(1)} %copy-done.12, bf16[4608,512]{1,0:T(8,128)(2,1)} %param.20, bf16[512,4608]{1,0:T(8,128)(2,1)S(1)} %fusion.3, f32[4608]{0:T(1024)S(1)} %copy-done.9), kind=kOutput, calls=%fused_computation.32 | convolution fusion | flops 2424045056 | bytes 10508288 | tf_op jit(solution)/shard_map/dot_general | solution.py:104
  263.7 5.1 %fusion.39 = f32[512,4608]{1,0:T(8,128)} fusion(bf16[512,4608]{1,0:T(8,128)(2,1)S(1)} %bitcast.41, f32[512,512]{1,0:T(8,128)S(1)} %get-tuple-element.25), kind=kOutput, calls=%fused_computation.69 | convolution fusion | flops 2416443392 | bytes 15204352 | tf_op jit(solution)/shard_map/dot_general | solution.py:109
  268.8 0.0 all-reduce.5.cloned.1.call-update
  268.8 3.3 fusion.5
  272.2 0.6 multiply_reduce_fusion.1
  272.8 65.8 %psum.55 = f32[]{:T(128)} all-reduce(f32[]{:T(128)} %get-tuple-element.16), channel_id=1, replica_groups=mesh['heads'=8,'width'=4,'sae'=4] {'heads','width','sae'}, use_global_device_ids=true, to_apply=%region_15.16 | all-reduce | flops 1 | bytes 8 | tf_op jit(solution)/shard_map/psum | solution.py:113
  339.2 94.4 %all-reduce.5.cloned.1.call-done = f32[512,4608]{1,0:T(8,128)} async-done(((f32[512,4608]{1,0:T(8,128)}), f32[512,4608]{1,0:T(8,128)}) %all-reduce.5.cloned.1.call-update) | async-done | bytes 9437200 | tf_op jit(solution)/shard_map/psum | solution.py:110
  433.6 8.4 %multiply_reduce_fusion = (f32[]{:T(128)}, bf16[512,4608]{1,0:T(8,128)(2,1)S(1)}) fusion(bf16[512,4608]{1,0:T(8,128)(2,1)} %copy-done.2, f32[512,4608]{1,0:T(8,128)} %all-reduce.5.cloned.1.call-done, f32[4608]{0:T(1024)S(1)} %copy-done.9), kind=kLoop, calls=%fused_computation.15 | loop fusion | flops 16515071 | bytes 18892804 | tf_op jit(solution)/shard_map/reduce_sum | solution.py:112
  442.0 6.7 %fusion.20 = bf16[512,512]{1,0:T(8,128)(2,1)S(1)} fusion(bf16[512,4608]{1,0:T(8,128)(2,1)S(1)} %get-tuple-element.7, bf16[512,4608]{1,0:T(8,128)(2,1)} %param.22, f32[512,512]{1,0:T(8,128)S(1)} %get-tuple-element.25, f32[512]{0:T(512)S(1)} %get-tuple-element.17), kind=kOutput, calls=%fused_computation.30 | convolution fusion | flops 2416967680 | bytes 11012096 | tf_op jit(solution)/shard_map/dot_general | solution.py:116
  448.7 6.8 %convolution_convert_fusion = bf16[4608,512]{1,0:T(8,128)(2,1)} fusion(bf16[512,512]{1,0:T(8,128)(2,1)S(1)} %fusion.20, bf16[512,4608]{1,0:T(8,128)(2,1)} %copy-done.2, f32[4608]{0:T(1024)S(1)} %copy-done.9), kind=kOutput, calls=%fused_computation.17 | convolution fusion | flops 2425356288 | bytes 9979904 | tf_op jit(solution)/shard_map/dot_general | solution.py:122
  456.1 7.8 %fusion.8 = bf16[512,4608]{1,0:T(8,128)(2,1)} fusion(bf16[512,4608]{1,0:T(8,128)(2,1)} %param.22, bf16[512,4608]{1,0:T(8,128)(2,1)} %copy-done.4, f32[512]{0:T(512)S(1)} %get-tuple-element.18, f32[512]{0:T(512)S(1)} %get-tuple-element.19, f32[512,512]{1,0:T(8,128)S(1)} %get-tuple-element.25), kind=kOutput, calls=%fused_computation.14 | convolution fusion | flops 2428239872 | bytes 15208448 | tf_op jit(solution)/shard_map/dot_general | solution.py:125
  (35 shorter events, 0.1 us)
Async XLA Ops:
  7.2 83.3 %copy-start = (bf16[512,1152]{1,0:T(8,128)(2,1)S(1)}, bf16[512,1152]{1,0:T(8,128)(2,1)}, u32[]{:S(2)}) copy-start(bf16[512,1152]{1,0:T(8,128)(2,1)} %param.18) | copy-start | bytes 3538948
  7.2 6.5 %copy-start.3 = (bf16[512,1152]{1,0:T(8,128)(2,1)S(1)}, bf16[512,1152]{1,0:T(8,128)(2,1)}, u32[]{:S(2)}) copy-start(bf16[512,1152]{1,0:T(8,128)(2,1)} %param.12) | copy-start | bytes 3538948
  7.2 6.4 %copy-start.11 = (f32[1152]{0:T(1024)S(1)}, f32[1152]{0:T(1024)}, u32[]{:S(2)}) copy-start(f32[1152]{0:T(1024)} %param.14) | copy-start | bytes 13828
  7.2 6.4 %copy-start.10 = (bf16[1152,256]{1,0:T(8,128)(2,1)S(1)}, bf16[1152,256]{1,0:T(8,128)(2,1)}, u32[]{:S(2)}) copy-start(bf16[1152,256]{1,0:T(8,128)(2,1)} %param.17) | copy-start | bytes 1769476
  7.2 7.8 %copy-start.13 = (s32[4]{0:T(128)S(1)}, s32[4]{0:T(128)}, u32[]{:S(2)}) copy-start(s32[4]{0:T(128)} %param.13) | copy-start | bytes 52
  7.2 69.6 %all-reduce.7.cloned.1.call-start = ((), (), s32[]{:S(2)}) async-start(), calls=%async_computation.3 | async-start | bytes 4194304 | tf_op jit(solution)/shard_map/psum | solution.py:73
  15.0 181.6 %all-gather.5.cloned.1.call-start = ((), (), s32[]{:S(2)}) async-start(), calls=%async_computation.1 | async-start | bytes 5898240 | tf_op jit(solution)/shard_map/all_gather | solution.py:95
  82.4 2.0 copy-start.6
  82.4 2.1 copy-start.5
  85.9 2.9 copy-start.7
  91.3 160.0 %copy-start.8 = (f32[4608]{0:T(1024)S(1)}, f32[4608]{0:T(1024)}, u32[]{:S(2)}) copy-start(f32[4608]{0:T(1024)} %param.19) | copy-start | bytes 55300
  143.8 107.5 %all-gather.3.cloned.1.call-start = ((), (), s32[]{:S(2)}) async-start(), calls=%async_computation | async-start | bytes 5898240 | tf_op jit(solution)/shard_map/all_gather | solution.py:96
  144.5 289.1 %all-reduce.5.cloned.1.call-start = ((), (), s32[]{:S(2)}) async-start(), calls=%async_computation.2 | async-start | bytes 18874368 | tf_op jit(solution)/shard_map/psum | solution.py:110
  199.9 57.3 %copy-start.9 = (f32[4608]{0:T(1024)S(1)}, f32[4608]{0:T(1024)}, u32[]{:S(2)}) copy-start(f32[4608]{0:T(1024)} %param.23) | copy-start | bytes 55300
  199.9 57.3 %copy-start.12 = (f32[512]{0:T(512)S(1)}, f32[512]{0:T(512)}, u32[]{:S(2)}) copy-start(f32[512]{0:T(512)} %param.21) | copy-start | bytes 6148
  251.3 12.4 %slice-start = ((s8[4718592]{0:T(1024)(128)(4,1)}), s8[4194304]{0:T(1024)(128)(4,1)S(1)}, s32[]{:S(2)}) async-start(s8[4718592]{0:T(1024)(128)(4,1)} %bitcast.40), calls=%async_computation.4 | async-start | bytes 8388608
  257.2 6.4 %copy-start.2 = (bf16[512,4608]{1,0:T(8,128)(2,1)}, bf16[512,4608]{1,0:T(8,128)(2,1)S(1)}, u32[]{:S(2)}) copy-start(bf16[512,4608]{1,0:T(8,128)(2,1)S(1)} %fusion.3) | copy-start | bytes 14155780
  257.2 6.5 %slice-start.1 = ((s8[4718592]{0:T(1024)(128)(4,1)}), s8[524288]{0:T(1024)(128)(4,1)S(1)}, s32[]{:S(2)}) async-start(s8[4718592]{0:T(1024)(128)(4,1)} %bitcast.40), calls=%async_computation.5 | async-start | bytes 1048576
  442.0 6.7 %copy-start.4 = (bf16[512,4608]{1,0:T(8,128)(2,1)}, bf16[512,4608]{1,0:T(8,128)(2,1)S(1)}, u32[]{:S(2)}) copy-start(bf16[512,4608]{1,0:T(8,128)(2,1)S(1)} %get-tuple-element.7) | copy-start | bytes 14155780
  456.1 7.9 %copy-start.1 = (bf16[512,1152]{1,0:T(8,128)(2,1)S(1)}, bf16[512,1152]{1,0:T(8,128)(2,1)}, u32[]{:S(2)}) copy-start(bf16[512,1152]{1,0:T(8,128)(2,1)} %param.18) | copy-start | bytes 3538948
Sparse Core Ops, SparseCore 0:
  15.1 61.7 all-reduce.6
  143.9 52.6 all-gather.4
  198.3 52.9 all-gather.2
  268.9 164.6 all-reduce.4
where the time goes:
time: 472 us
  waiting for transfers between devices  247 us (52%)
  blocking collectives  128 us (27%)
  matrix products  45.7 us (10%)
  other arithmetic  31.4 us (7%)
  between operations  16.5 us (3%)
    psum x1, waiting for transfers between devices, per_device(): recon = lax.psum(recon_part, ('heads', 'width', 'sae')) + dec_bias  94.4 us
    psum x1, blocking collectives, per_device(): penalty_total = lax.psum(penalty_part, ('heads', 'width', 'sae'))  65.8 us
    psum x1, blocking collectives, per_device(): attn_sum = lax.psum(proj_part, 'heads')  52.5 us
    all_gather x1, waiting for transfers between devices, per_device(): lax.all_gather(attn_local, 'width', axis=1, tiled=True)  51.8 us
    all_gather x1, waiting for transfers between devices, per_device(): lax.all_gather(x_in, 'width', axis=1, tiled=True)  51.3 us
    psum x1, waiting for transfers between devices, per_device(): lax.psum((query_part, key_part, value_part, square_part), 'width')  49 us
    psum x1, blocking collectives, per_device(): lax.psum((query_part, key_part, value_part, square_part), 'width')  9.54 us
  transfers between devices with their start and end apart: 4, of which 4 were waited for; matrix products, arithmetic and copies ran while one was open for 2% of the time, Pallas kernels for 0%

commit v1 on v0

--- a/solution.py
+++ b/solution.py
@@ -93,7 +93,7 @@
     attn_local = attn_sum.astype(jnp.bfloat16)
     attn_proj, x_full = (
         lax.all_gather(attn_local, "width", axis=1, tiled=True),
-        lax.all_gather(x_in, "width", axis=1, tiled=True),
+        jnp.concatenate(lax.all_gather(x_in, "width"), axis=1),
     )
     proj_float = attn_proj.astype(jnp.float32)
     inverse_post = lax.rsqrt(jnp.sum(proj_float * proj_float, axis=1) / D + norm_eps)

time: 472 us -> 423 us (0.90)
  waiting for transfers between devices: 247 us -> 178 us
  local copies, waits for them, and re-layouts: 2.52 us -> 22 us
    all_gather x1, waiting for transfers between devices: 51.3 us -> 0.02 us  [per_device(): lax.all_gather(x_in, 'width')]
    all_gather x1, waiting for transfers between devices: 51.8 us -> 33.6 us  [per_device(): lax.all_gather(attn_local, 'width', axis=1, tiled=True)]
    convert_element_type x0 -> x1, local copies, waits for them, and re-layouts: none -> 9.77 us  [per_device(): x_full.astype(jnp.float32) + proj_float * inverse_post[:, None] * post_gain]
    unnamed x32 -> x33, local copies, waits for them, and re-layouts: 0.09 us -> 8.82 us
  transfers between devices with their start and end apart: 4 -> 4, of which waited for: 4 -> 3; matrix products, arithmetic and copies ran while one was open for 2% -> 9% of each run, Pallas kernels for 0% -> 0%
where the time goes in v1:
time: 423 us; the launch traced here: 422 us
  waiting for transfers between devices  178 us (42%)
  blocking collectives  130 us (31%)
  matrix products  45.4 us (11%)
  other arithmetic  30.7 us (7%)
  local copies, waits for them, and re-layouts  22 us (5%)
  between operations  16.4 us (4%)
    psum x1, waiting for transfers between devices, per_device(): recon = lax.psum(recon_part, ('heads', 'width', 'sae')) + dec_bias  94.3 us
    psum x1, blocking collectives, per_device(): penalty_total = lax.psum(penalty_part, ('heads', 'width', 'sae'))  65.8 us
    psum x1, blocking collectives, per_device(): attn_sum = lax.psum(proj_part, 'heads')  54.5 us
    psum x1, waiting for transfers between devices, per_device(): lax.psum((query_part, key_part, value_part, square_part), 'width')  49 us
    all_gather x1, waiting for transfers between devices, per_device(): lax.all_gather(attn_local, 'width', axis=1, tiled=True)  33.6 us
    convert_element_type x1, local copies, waits for them, and re-layouts, per_device(): x_full.astype(jnp.float32) + proj_float * inverse_post[:, None] * post_gain  9.77 us
    psum x1, blocking collectives, per_device(): lax.psum((query_part, key_part, value_part, square_part), 'width')  9.55 us
    unnamed x33, local copies, waits for them, and re-layouts  8.82 us
  transfers between devices with their start and end apart: 4, of which 3 were waited for; matrix products, arithmetic and copies ran while one was open for 9% of the time, Pallas kernels for 0%

profile of v1, /device:TPU:1, one launch (start us, length us, event | category | flops | bytes accessed | tf_op | source)
XLA Modules:
  0.0 422.4 jit_solution(1412428543357622694)
XLA Ops:
  7.2 0.0 all-reduce.7.cloned.1.call-start
  7.3 3.6 fusion.23
  10.9 2.8 fusion.25
  13.7 1.3 fusion.27
  15.0 0.0 all-reduce.7.cloned.1.call-update
  15.1 0.0 all-gather.6.cloned.1.call-start
  15.1 0.7 all-gather.6.cloned.1.call-update
  15.8 0.0 all-gather.4.cloned.1.call-start
  15.9 0.2 reduce-window.8
  16.0 0.3 fusion.14
  16.4 9.5 %psum.50 = f32[512]{0:T(512)S(1)} all-reduce(f32[512]{0:T(512)S(1)} %fusion.14), channel_id=1, replica_groups=mesh['heads'=8,'width'=4,'sae'=4] {'width'}, use_global_device_ids=true, to_apply=%region_2.3 | all-reduce | flops 512 | bytes 4096 | tf_op jit(solution)/shard_map/psum | solution.py:73
  25.9 0.1 convert_reduce_fusion.1
  26.0 0.9 fusion.22
  26.9 1.0 multiply_cosine_fusion
  27.9 49.0 %all-reduce.7.cloned.1.call-done = (f32[512,256]{1,0:T(8,128)}, f32[512,512]{1,0:T(8,128)}, f32[512,256]{1,0:T(8,128)}) async-done(((f32[512,256]{1,0:T(8,128)}, f32[512,512]{1,0:T(8,128)}, f32[512,256]{1,0:T(8,128)}), (f32[512,256]{1,0:T(8,128)}, f32[512,512]{1,0:T(8,128)}, f32[512,256]{1,0:T(8,128)})) %all-reduce.7.cloned.1.call-update) | async-done | bytes 2097168 | tf_op jit(solution)/shard_map/psum | solution.py:73
  76.9 1.3 broadcast_multiply_fusion.1
  78.3 0.3 reshape.172
  78.6 2.3 broadcast_multiply_fusion
  80.9 1.6 reshape.173
  82.5 0.8 subtract_convert_fusion
  83.3 0.1 copy.26
  83.3 0.1 copy.25
  83.4 0.8 copy.32
  84.3 0.6 fusion.40
  84.9 0.1 subtract_convert_fusion.1
  85.0 2.9 fusion.12
  87.9 1.6 fusion.21
  89.5 0.9 fusion.41
  90.4 54.5 %all-reduce.8 = bf16[512,1152]{1,0:T(8,128)(2,1)} all-reduce(f32[512,1152]{1,0:T(8,128)S(1)} %fusion.41), channel_id=1, replica_groups=mesh['heads'=8,'width'=4,'sae'=4] {'heads'}, use_global_device_ids=true, to_apply=%region_8.9 | all-reduce | flops 589824 | bytes 3538944 | tf_op jit(solution)/shard_map/psum | solution.py:92
  144.8 0.0 all-gather.4.cloned.1.call-update
  144.9 0.2 all-reduce.5.cloned.1.call-start
  145.1 0.0 all-gather.6.cloned.1.call-done
  145.1 9.8 %copy.22 = f32[4,512,1152]{2,0,1:T(4,128)} copy(bf16[4,512,1152]{2,1,0:T(8,128)(2,1)} %bitcast.49) | data formatting | bytes 14155776 | tf_op jit(solution)/shard_map/convert_element_type | solution.py:100
  154.9 8.5 %copy.35 = f32[64,8,4,1152]{3,1,2,0:T(8,128)} copy(f32[64,8,4,1152]{3,2,1,0:T(4,128)} %bitcast.46) | data formatting | bytes 18874368
  163.4 33.6 %all-gather.4.cloned.1.call-done = bf16[512,4608]{1,0:T(8,128)(2,1)} async-done(((bf16[512,1152]{1,0:T(8,128)(2,1)}), bf16[512,4608]{1,0:T(8,128)(2,1)}) %all-gather.4.cloned.1.call-update) | async-done | bytes 4718608 | tf_op jit(solution)/shard_map/all_gather | solution.py:95
  197.0 3.5 fusion
  200.5 0.3 copy-done.2
  200.7 7.8 %fusion.3 = bf16[512,4608]{1,0:T(8,128)(2,1)} fusion(f32[512,4608]{1,0:T(8,128)} %bitcast.45, bf16[512,4608]{1,0:T(8,128)(2,1)S(1)} %copy-done.2, f32[4608]{0:T(1024)S(1)} %copy-done.8, f32[512]{0:T(512)S(1)} %add_rsqrt_fusion), kind=kLoop, calls=%fused_computation.9 | loop fusion | flops 11796480 | bytes 18894848 | tf_op jit(solution)/shard_map/convert_element_type | solution.py:100
  208.6 6.0 %convert_reduce_fusion = (f32[512]{0:T(512)S(1)}, f32[512,512]{1,0:T(8,128)S(1)}) fusion(f32[512]{0:T(512)S(1)} %copy-done.12, bf16[4608,512]{1,0:T(8,128)(2,1)} %param.20, bf16[512,4608]{1,0:T(8,128)(2,1)} %fusion.3, f32[4608]{0:T(1024)S(1)} %copy-done.9), kind=kOutput, calls=%fused_computation.32 | convolution fusion | flops 2424045056 | bytes 10508288 | tf_op jit(solution)/shard_map/dot_general | solution.py:104
  214.6 5.1 %fusion.39 = f32[512,4608]{1,0:T(8,128)} fusion(bf16[512,4608]{1,0:T(8,128)(2,1)S(1)} %bitcast.48, f32[512,512]{1,0:T(8,128)S(1)} %get-tuple-element.25), kind=kOutput, calls=%fused_computation.69 | convolution fusion | flops 2416443392 | bytes 15204352 | tf_op jit(solution)/shard_map/dot_general | solution.py:109
  219.7 3.3 fusion.5
  223.1 0.6 multiply_reduce_fusion.1
  223.7 65.8 %psum.55 = f32[]{:T(128)} all-reduce(f32[]{:T(128)} %get-tuple-element.16), channel_id=1, replica_groups=mesh['heads'=8,'width'=4,'sae'=4] {'heads','width','sae'}, use_global_device_ids=true, to_apply=%region_15.16 | all-reduce | flops 1 | bytes 8 | tf_op jit(solution)/shard_map/psum | solution.py:113
  290.1 94.3 %all-reduce.5.cloned.1.call-done = f32[512,4608]{1,0:T(8,128)} async-done(((f32[512,4608]{1,0:T(8,128)}), f32[512,4608]{1,0:T(8,128)}) %all-reduce.5.cloned.1.call-update) | async-done | bytes 9437200 | tf_op jit(solution)/shard_map/psum | solution.py:110
  384.4 8.4 %multiply_reduce_fusion = (f32[]{:T(128)}, bf16[512,4608]{1,0:T(8,128)(2,1)S(1)}) fusion(bf16[512,4608]{1,0:T(8,128)(2,1)} %fusion.3, f32[512,4608]{1,0:T(8,128)} %all-reduce.5.cloned.1.call-done, f32[4608]{0:T(1024)S(1)} %copy-done.9), kind=kLoop, calls=%fused_computation.15 | loop fusion | flops 16515071 | bytes 18892804 | tf_op jit(solution)/shard_map/reduce_sum | solution.py:112
  392.8 6.7 %fusion.20 = bf16[512,512]{1,0:T(8,128)(2,1)S(1)} fusion(bf16[512,4608]{1,0:T(8,128)(2,1)S(1)} %get-tuple-element.7, bf16[512,4608]{1,0:T(8,128)(2,1)} %param.22, f32[512,512]{1,0:T(8,128)S(1)} %get-tuple-element.25, f32[512]{0:T(512)S(1)} %get-tuple-element.17), kind=kOutput, calls=%fused_computation.30 | convolution fusion | flops 2416967680 | bytes 11012096 | tf_op jit(solution)/shard_map/dot_general | solution.py:116
  399.5 6.7 %convolution_convert_fusion = bf16[4608,512]{1,0:T(8,128)(2,1)} fusion(bf16[512,512]{1,0:T(8,128)(2,1)S(1)} %fusion.20, bf16[512,4608]{1,0:T(8,128)(2,1)} %fusion.3, f32[4608]{0:T(1024)S(1)} %copy-done.9), kind=kOutput, calls=%fused_computation.17 | convolution fusion | flops 2425356288 | bytes 9979904 | tf_op jit(solution)/shard_map/dot_general | solution.py:122
  406.9 7.8 %fusion.8 = bf16[512,4608]{1,0:T(8,128)(2,1)} fusion(bf16[512,4608]{1,0:T(8,128)(2,1)} %param.22, bf16[512,4608]{1,0:T(8,128)(2,1)} %copy-done.5, f32[512]{0:T(512)S(1)} %get-tuple-element.18, f32[512]{0:T(512)S(1)} %get-tuple-element.19, f32[512,512]{1,0:T(8,128)S(1)} %get-tuple-element.25), kind=kOutput, calls=%fused_computation.14 | convolution fusion | flops 2428239872 | bytes 15208448 | tf_op jit(solution)/shard_map/dot_general | solution.py:125
  (37 shorter events, 0.1 us)
Async XLA Ops:
  7.2 82.3 %copy-start = (bf16[512,1152]{1,0:T(8,128)(2,1)S(1)}, bf16[512,1152]{1,0:T(8,128)(2,1)}, u32[]{:S(2)}) copy-start(bf16[512,1152]{1,0:T(8,128)(2,1)} %param.18) | copy-start | bytes 3538948
  7.2 6.5 %copy-start.3 = (bf16[512,1152]{1,0:T(8,128)(2,1)S(1)}, bf16[512,1152]{1,0:T(8,128)(2,1)}, u32[]{:S(2)}) copy-start(bf16[512,1152]{1,0:T(8,128)(2,1)} %param.12) | copy-start | bytes 3538948
  7.2 6.5 %copy-start.11 = (f32[1152]{0:T(1024)S(1)}, f32[1152]{0:T(1024)}, u32[]{:S(2)}) copy-start(f32[1152]{0:T(1024)} %param.14) | copy-start | bytes 13828
  7.2 69.7 %all-reduce.7.cloned.1.call-start = ((), (), s32[]{:S(2)}) async-start(), calls=%async_computation.3 | async-start | bytes 4194304 | tf_op jit(solution)/shard_map/psum | solution.py:73
  7.3 6.5 %copy-start.10 = (bf16[1152,256]{1,0:T(8,128)(2,1)S(1)}, bf16[1152,256]{1,0:T(8,128)(2,1)}, u32[]{:S(2)}) copy-start(bf16[1152,256]{1,0:T(8,128)(2,1)} %param.17) | copy-start | bytes 1769476
  10.9 5.0 %copy-start.13 = (s32[4]{0:T(128)S(1)}, s32[4]{0:T(128)}, u32[]{:S(2)}) copy-start(s32[4]{0:T(128)} %param.13) | copy-start | bytes 52
  10.9 5.2 %copy-start.4 = (bf16[512,1152]{1,0:T(8,128)(2,1)S(1)}, bf16[512,1152]{1,0:T(8,128)(2,1)}, u32[]{:S(2)}) copy-start(bf16[512,1152]{1,0:T(8,128)(2,1)} %param.12) | copy-start | bytes 3538948
  15.1 130.1 %all-gather.6.cloned.1.call-start = ((), (), s32[]{:S(2)}) async-start(), calls=%async_computation.2 | async-start | bytes 5898240 | tf_op jit(solution)/shard_map/all_gather | solution.py:96
  15.8 181.2 %all-gather.4.cloned.1.call-start = ((), (), s32[]{:S(2)}) async-start(), calls=%async_computation | async-start | bytes 5898240 | tf_op jit(solution)/shard_map/all_gather | solution.py:95
  85.0 2.9 copy-start.6
  85.0 2.9 copy-start.7
  144.9 239.6 %all-reduce.5.cloned.1.call-start = ((), (), s32[]{:S(2)}) async-start(), calls=%async_computation.1 | async-start | bytes 18874368 | tf_op jit(solution)/shard_map/psum | solution.py:110
  154.9 45.6 %copy-start.8 = (f32[4608]{0:T(1024)S(1)}, f32[4608]{0:T(1024)}, u32[]{:S(2)}) copy-start(f32[4608]{0:T(1024)} %param.19) | copy-start | bytes 55300
  197.0 3.8 copy-start.2
  200.7 7.8 %copy-start.9 = (f32[4608]{0:T(1024)S(1)}, f32[4608]{0:T(1024)}, u32[]{:S(2)}) copy-start(f32[4608]{0:T(1024)} %param.23) | copy-start | bytes 55300
  200.7 7.8 %copy-start.12 = (f32[512]{0:T(512)S(1)}, f32[512]{0:T(512)}, u32[]{:S(2)}) copy-start(f32[512]{0:T(512)} %param.21) | copy-start | bytes 6148
  200.7 13.9 %slice-start = ((s8[4718592]{0:T(1024)(128)(4,1)}), s8[524288]{0:T(1024)(128)(4,1)S(1)}, s32[]{:S(2)}) async-start(s8[4718592]{0:T(1024)(128)(4,1)} %bitcast.47), calls=%async_computation.4 | async-start | bytes 1048576
  208.6 6.1 %slice-start.1 = ((s8[4718592]{0:T(1024)(128)(4,1)}), s8[4194304]{0:T(1024)(128)(4,1)S(1)}, s32[]{:S(2)}) async-start(s8[4718592]{0:T(1024)(128)(4,1)} %bitcast.47), calls=%async_computation.5 | async-start | bytes 8388608
  392.8 6.7 %copy-start.5 = (bf16[512,4608]{1,0:T(8,128)(2,1)}, bf16[512,4608]{1,0:T(8,128)(2,1)S(1)}, u32[]{:S(2)}) copy-start(bf16[512,4608]{1,0:T(8,128)(2,1)S(1)} %get-tuple-element.7) | copy-start | bytes 14155780
  406.9 7.9 %copy-start.1 = (bf16[512,1152]{1,0:T(8,128)(2,1)S(1)}, bf16[512,1152]{1,0:T(8,128)(2,1)}, u32[]{:S(2)}) copy-start(bf16[512,1152]{1,0:T(8,128)(2,1)} %param.18) | copy-start | bytes 3538948
Sparse Core Ops, SparseCore 0:
  15.2 61.7 all-reduce.6
  78.6 52.3 all-gather.5
  145.0 51.9 all-gather.3
  219.8 164.5 all-reduce.4
